TPU v7x, 512 devices: a whole 4x4x16 slice. The times are simulated.
512 devices in a mesh: shard: 64 (over z, x), tensor: 4 (over y), section: 2 (over core).
Axes of the slice: x: 4, y: 4, z: 16, core: 2. Of those that a mesh axis runs over, the one named last changes fastest.
Arguments:
- query_key: float32 [2, 2, 1024, 1024], P('section', None, 'shard', 'tensor'), may hold values from -52 to 52, as said below
- query_key_gradient: float32 [2, 2, 1024, 1024], P('section', None, 'shard', 'tensor'), may hold values from -52 to 52
- query_key_first: float32 [2, 2, 1024, 1024], P('section', None, 'shard', 'tensor'), may hold values from -5.2 to 5.2
- query_key_second: float32 [2, 2, 1024, 1024], P('section', None, 'shard', 'tensor'), may hold values from 0.01 to 1
- value_gate: float32 [2, 2, 1024, 2048], P('section', None, 'shard', 'tensor'), may hold values from -52 to 52
- value_gate_gradient: float32 [2, 2, 1024, 2048], P('section', None, 'shard', 'tensor'), may hold values from -52 to 52
- value_gate_first: float32 [2, 2, 1024, 2048], P('section', None, 'shard', 'tensor'), may hold values from -5.2 to 5.2
- value_gate_second: float32 [2, 2, 1024, 2048], P('section', None, 'shard', 'tensor'), may hold values from 0.01 to 1
- output_weight: float32 [2, 2048, 1024], P('section', 'tensor', 'shard'), may hold values from -52 to 52
- output_gradient: float32 [2, 2048, 1024], P('section', 'tensor', 'shard'), may hold values from -52 to 52
- output_first: float32 [2, 2048, 1024], P('section', 'tensor', 'shard'), may hold values from -5.2 to 5.2
- output_second: float32 [2, 2048, 1024], P('section', 'tensor', 'shard'), may hold values from 0.01 to 1
- norm_gain: float32 [2, 1024], P('section', 'shard'), may hold values from -52 to 52
- gain_gradient: float32 [2, 1024], P('section', 'shard'), may hold values from -52 to 52
- gain_first: float32 [2, 1024], P('section', 'shard'), may hold values from -5.2 to 5.2
- gain_second: float32 [2, 1024], P('section', 'shard'), may hold values from 0.01 to 1
Outputs:
- new_query_key: float32 [2, 2, 1024, 1024], P('section', None, 'shard', 'tensor')
- new_query_key_first: float32 [2, 2, 1024, 1024], P('section', None, 'shard', 'tensor')
- new_query_key_second: float32 [2, 2, 1024, 1024], P('section', None, 'shard', 'tensor')
- new_value_gate: float32 [2, 2, 1024, 2048], P('section', None, 'shard', 'tensor')
- new_value_gate_first: float32 [2, 2, 1024, 2048], P('section', None, 'shard', 'tensor')
- new_value_gate_second: float32 [2, 2, 1024, 2048], P('section', None, 'shard', 'tensor')
- new_output: float32 [2, 2048, 1024], P('section', 'tensor', 'shard')
- new_output_first: float32 [2, 2048, 1024], P('section', 'tensor', 'shard')
- new_output_second: float32 [2, 2048, 1024], P('section', 'tensor', 'shard')
- new_gain: float32 [2, 1024], P('section', 'shard')
- new_gain_first: float32 [2, 1024], P('section', 'shard')
- new_gain_second: float32 [2, 1024], P('section', 'shard')
- copy_query_key: bfloat16 [2, 2, 1024, 1024], P('section', None, None, 'tensor')
- copy_value_gate: bfloat16 [2, 2, 1024, 2048], P('section', None, None, 'tensor')
- copy_output: bfloat16 [2, 2048, 1024], P('section', 'tensor')
- copy_gain: bfloat16 [2, 1024], P('section')
Inputs may be any that keep to these rules, and one draw needn't show every extreme that they name: `query_key`: projection weights, gradients and first moments are real-valued with entries of differing scale.
All inputs are finite; a program needn't handle non-finite values.
Results may differ from a plain program's by a relative error of at most 0.001.
Values may be sent and summed in bfloat16 or wider, within the bound.
A program may use at most 64 MiB of HBM per device.

v0:
```python
import jax
import jax.numpy as jnp
from jax import lax
from jax.sharding import PartitionSpec as P

STEP = 10
beta_one = 0.9
beta_two = 0.999
epsilon = 1e-06
learn_rate = 0.2


def local_terms(weight, gradient, first, second, decay, matrix_dims):
    first_new = beta_one * first + (1.0 - beta_one) * gradient
    second_new = beta_two * second + (1.0 - beta_two) * gradient * gradient
    update = (
        first_new
        / (1.0 - beta_one**STEP)
        / (jnp.sqrt(second_new / (1.0 - beta_two**STEP)) + epsilon)
        + decay * weight
    )
    norm_axes = tuple(range(weight.ndim - matrix_dims, weight.ndim))
    weight_sq = jnp.sum(weight * weight, axis=norm_axes)
    update_sq = jnp.sum(update * update, axis=norm_axes)
    return (first_new, second_new, update, weight_sq, update_sq)


def apply_trust(weight, update, weight_sq, update_sq, matrix_dims):
    trust = jnp.sqrt(weight_sq) / (jnp.sqrt(update_sq) + epsilon)
    trust = trust.reshape(trust.shape + (1,) * matrix_dims)
    return weight - learn_rate * trust * update


def on_device(
    query_key,
    query_key_gradient,
    query_key_first,
    query_key_second,
    value_gate,
    value_gate_gradient,
    value_gate_first,
    value_gate_second,
    output_weight,
    output_gradient,
    output_first,
    output_second,
    norm_gain,
    gain_gradient,
    gain_first,
    gain_second,
):
    qk_terms = local_terms(
        query_key, query_key_gradient, query_key_first, query_key_second, 0.01, 2
    )
    vg_terms = local_terms(
        value_gate, value_gate_gradient, value_gate_first, value_gate_second, 0.01, 2
    )
    output_terms = local_terms(output_weight, output_gradient, output_first, output_second, 0.01, 2)
    gain_terms = local_terms(norm_gain, gain_gradient, gain_first, gain_second, 0.0, 1)
    qk_sq = lax.psum((qk_terms[3], qk_terms[4]), ("shard", "tensor"))
    vg_sq = lax.psum((vg_terms[3], vg_terms[4]), ("shard", "tensor"))
    output_sq = lax.psum((output_terms[3], output_terms[4]), ("shard", "tensor"))
    gain_sq = lax.psum((gain_terms[3], gain_terms[4]), "shard")
    new_qk = apply_trust(query_key, qk_terms[2], qk_sq[0], qk_sq[1], 2)
    new_vg = apply_trust(value_gate, vg_terms[2], vg_sq[0], vg_sq[1], 2)
    new_output = apply_trust(output_weight, output_terms[2], output_sq[0], output_sq[1], 2)
    new_gain = apply_trust(norm_gain, gain_terms[2], gain_sq[0], gain_sq[1], 1)
    qk_half = new_qk.astype(jnp.bfloat16)
    vg_half = new_vg.astype(jnp.bfloat16)
    output_half = new_output.astype(jnp.bfloat16)
    gain_half = new_gain.astype(jnp.bfloat16)
    copy_qk = lax.all_gather(qk_half, "shard", axis=2, tiled=True)
    copy_vg = lax.all_gather(vg_half, "shard", axis=2, tiled=True)
    copy_output = lax.all_gather(output_half, "shard", axis=2, tiled=True)
    copy_gain = lax.all_gather(gain_half, "shard", axis=1, tiled=True)
    return (
        new_qk,
        qk_terms[0],
        qk_terms[1],
        new_vg,
        vg_terms[0],
        vg_terms[1],
        new_output,
        output_terms[0],
        output_terms[1],
        new_gain,
        gain_terms[0],
        gain_terms[1],
        copy_qk,
        copy_vg,
        copy_output,
        copy_gain,
    )


def solution(mesh):
    placed = (
        P("section", None, "shard", "tensor"),
        P("section", None, "shard", "tensor"),
        P("section", None, "shard", "tensor"),
        P("section", None, "shard", "tensor"),
        P("section", None, "shard", "tensor"),
        P("section", None, "shard", "tensor"),
        P("section", None, "shard", "tensor"),
        P("section", None, "shard", "tensor"),
        P("section", "tensor", "shard"),
        P("section", "tensor", "shard"),
        P("section", "tensor", "shard"),
        P("section", "tensor", "shard"),
        P("section", "shard"),
        P("section", "shard"),
        P("section", "shard"),
        P("section", "shard"),
    )
    return jax.shard_map(
        on_device,
        mesh=mesh,
        in_specs=placed,
        out_specs=(
            P("section", None, "shard", "tensor"),
            P("section", None, "shard", "tensor"),
            P("section", None, "shard", "tensor"),
            P("section", None, "shard", "tensor"),
            P("section", None, "shard", "tensor"),
            P("section", None, "shard", "tensor"),
            P("section", "tensor", "shard"),
            P("section", "tensor", "shard"),
            P("section", "tensor", "shard"),
            P("section", "shard"),
            P("section", "shard"),
            P("section", "shard"),
            P("section", None, None, "tensor"),
            P("section", None, None, "tensor"),
            P("section", "tensor", None),
            P("section", None),
        ),
        check_vma=False,
    )
```

profile of v0, /device:TPU:8, one launch (start us, length us, event | category | flops | bytes accessed | tf_op | source)
XLA Modules:
  0.0 1120.5 jit_solution(3101346954064736465)
XLA Ops:
  7.2 0.0 all-gather.4.cloned.1.call-start
  7.2 1.1 multiply_reduce_fusion.1
  8.3 1.0 multiply_reduce_fusion.5
  9.3 1.5 multiply_reduce_fusion.2
  10.8 691.5 %all-reduce.1 = (f32[1,2]{1,0:T(1,128)S(1)}, f32[1,2]{1,0:T(1,128)S(1)}, f32[1,2]{1,0:T(1,128)S(1)}, f32[1,2]{1,0:T(1,128)S(1)}, f32[1]{0:T(128)}, /*index=5*/f32[1]{0:T(128)}) all-reduce(f32[1,2]{1,0:T(1,128)S(1)} %bitcast.20, f32[1,2]{1,0:T(1,128)S(1)} %bitcast.19, ...), channel_id=1, replica_groups=mesh['shard'=64,'tensor'=4,'section'=2] {'shard','tensor'}, use_global_device_ids=true, to_apply=%region_3.0 | all-reduce | flops 10 | bytes 80 | tf_op jit(solution)/shard_map/psum | solution.py:60
  702.3 1.5 fusion.6
  703.8 0.0 all-gather.4.cloned.1.call-update
  703.8 0.0 all-gather.8.cloned.1.call-start
  705.2 1.4 fusion.4
  706.6 0.0 all-gather.8.cloned.1.call-update
  706.7 0.0 all-gather.6.cloned.1.call-start
  706.7 1.6 fusion.5
  708.3 1.8 multiply_reduce_fusion.6
  710.1 138.7 %all-reduce.2 = (f32[1]{0:T(128)}, f32[1]{0:T(128)}) all-reduce(f32[1]{0:T(128)} %bitcast.9, f32[1]{0:T(128)} %bitcast.10), channel_id=1, replica_groups=mesh['shard'=64,'tensor'=4,'section'=2] {'shard'}, use_global_device_ids=true, to_apply=%region_13.0 | all-reduce | flops 2 | bytes 16 | tf_op jit(solution)/shard_map/psum | solution.py:63
  850.3 1.3 dynamic-slice
  852.2 1.2 convert_bitcast_fusion
  853.4 0.2 dynamic-update-slice
  853.5 140.4 %all-reduce = bf16[1024]{0:T(1024)(128)(2,1)S(1)} all-reduce(bf16[1024]{0:T(1024)(128)(2,1)S(1)} %dynamic-update-slice), channel_id=1, replica_groups=mesh['shard'=64,'tensor'=4,'section'=2] {'shard'}, use_global_device_ids=true, to_apply=%add | all-reduce | flops 1024 | bytes 4096
  993.9 0.6 reshape.78
  994.5 2.4 copy.33
  996.9 113.8 %all-gather.6.cloned.1.call-done = bf16[1,2,1024,512]{3,2,1,0:T(8,128)(2,1)} async-done(((bf16[1,2,16,512]{3,2,1,0:T(8,128)(2,1)}), bf16[1,2,1024,512]{3,2,1,0:T(8,128)(2,1)}) %all-gather.6.cloned.1.call-update) | async-done | bytes 2097168 | tf_op jit(solution)/shard_map/all_gather | solution.py:73
  1110.7 1.0 copy.37
  1111.7 1.0 copy-done
  1112.6 1.3 copy.38
  (20 shorter events, 0.1 us)
Async XLA Ops:
  7.2 987.3 %all-gather.4.cloned.1.call-start = ((), (), s32[]{:S(2)}) async-start(), calls=%async_computation | async-start | bytes 1064960 | tf_op jit(solution)/shard_map/all_gather | solution.py:72
  8.3 1103.3 %copy-start.2 = (f32[1,2,16,512]{3,2,1,0:T(8,128)}, f32[1,2,16,512]{3,2,1,0:T(8,128)S(1)}, u32[]{:S(2)}) copy-start(f32[1,2,16,512]{3,2,1,0:T(8,128)S(1)} %get-tuple-element.87) | copy-start | bytes 196612
  8.3 1103.3 %copy-start.3 = (f32[1,2,16,512]{3,2,1,0:T(8,128)}, f32[1,2,16,512]{3,2,1,0:T(8,128)S(1)}, u32[]{:S(2)}) copy-start(f32[1,2,16,512]{3,2,1,0:T(8,128)S(1)} %get-tuple-element.88) | copy-start | bytes 196612
  9.3 1102.3 %copy-start.4 = (f32[1,2,16,256]{3,2,1,0:T(8,128)}, f32[1,2,16,256]{3,2,1,0:T(8,128)S(1)}, u32[]{:S(2)}) copy-start(f32[1,2,16,256]{3,2,1,0:T(8,128)S(1)} %get-tuple-element.84) | copy-start | bytes 98308
  9.3 1102.3 %copy-start.5 = (f32[1,2,16,256]{3,2,1,0:T(8,128)}, f32[1,2,16,256]{3,2,1,0:T(8,128)S(1)}, u32[]{:S(2)}) copy-start(f32[1,2,16,256]{3,2,1,0:T(8,128)S(1)} %get-tuple-element.85) | copy-start | bytes 98308
  10.8 1100.9 %copy-start.6 = (f32[1,512,16]{1,2,0:T(8,128)}, f32[1,512,16]{1,2,0:T(8,128)S(1)}, u32[]{:S(2)}) copy-start(f32[1,512,16]{1,2,0:T(8,128)S(1)} %get-tuple-element.90) | copy-start | bytes 98308
  10.8 1100.9 %copy-start.7 = (f32[1,512,16]{1,2,0:T(8,128)}, f32[1,512,16]{1,2,0:T(8,128)S(1)}, u32[]{:S(2)}) copy-start(f32[1,512,16]{1,2,0:T(8,128)S(1)} %get-tuple-element.91) | copy-start | bytes 98308
  703.8 290.7 %all-gather.8.cloned.1.call-start = ((), (), s32[]{:S(2)}) async-start(), calls=%async_computation.2 | async-start | bytes 1064960 | tf_op jit(solution)/shard_map/all_gather | solution.py:74
  706.7 404.0 %all-gather.6.cloned.1.call-start = ((), (), s32[]{:S(2)}) async-start(), calls=%async_computation.1 | async-start | bytes 2129920 | tf_op jit(solution)/shard_map/all_gather | solution.py:73
  994.5 116.2 %copy-start.1 = (bf16[1,2,1024,256]{3,2,1,0:T(8,128)(2,1)S(1)}, bf16[1,2,1024,256]{3,2,1,0:T(8,128)(2,1)}, u32[]{:S(2)}) copy-start(bf16[1,2,1024,256]{3,2,1,0:T(8,128)(2,1)} %all-gather.4.cloned.1.call-done) | copy-start | bytes 3145732
  1110.7 2.0 copy-start
Sparse Core Ops, SparseCore 0:
  703.9 128.1 all-gather.3
  835.6 134.3 all-gather.7
  973.5 137.0 all-gather.5
where the time goes:
time: 1120 us
  blocking collectives  971 us (87%)
  waiting for transfers between devices  114 us (10%)
  between operations  17.3 us (2%)
    psum x1, blocking collectives, on_device(): qk_sq = lax.psum((qk_terms[3], qk_terms[4]), ('shard', 'tensor'))  691 us
    unnamed x1, blocking collectives  140 us
    psum x1, blocking collectives, on_device(): gain_sq = lax.psum((gain_terms[3], gain_terms[4]), 'shard')  139 us
    all_gather x1, waiting for transfers between devices, on_device(): copy_vg = lax.all_gather(vg_half, 'shard', axis=2, tiled=True)  114 us
  transfers between devices with their start and end apart: 3, of which 1 were waited for; matrix products, arithmetic and copies ran while one was open for 1% of the time, Pallas kernels for 0%

commit v1 on v0

--- a/solution.py
+++ b/solution.py
@@ -70,7 +70,9 @@
     output_half = new_output.astype(jnp.bfloat16)
     gain_half = new_gain.astype(jnp.bfloat16)
     copy_qk = lax.all_gather(qk_half, "shard", axis=2, tiled=True)
-    copy_vg = lax.all_gather(vg_half, "shard", axis=2, tiled=True)
+    copy_vg = jnp.concatenate(
+        lax.all_to_all(jnp.stack([vg_half] * lax.axis_size("shard")), "shard", 0, 0), axis=2
+    )
     copy_output = lax.all_gather(output_half, "shard", axis=2, tiled=True)
     copy_gain = lax.all_gather(gain_half, "shard", axis=1, tiled=True)
     return (

time: 1120 us -> 1060 us (0.946)
  the two profiles are of different devices: /device:TPU:8 before, /device:TPU:2 now
where the time goes in v1:
time: 1060 us
  blocking collectives  1010 us (95%)
  between operations  17.7 us (2%)
  starting transfers between devices  16.3 us (2%)
    psum x1, blocking collectives, on_device(): qk_sq = lax.psum((qk_terms[3], qk_terms[4]), ('shard', 'tensor'))  697 us
    psum x1, blocking collectives, on_device(): gain_sq = lax.psum((gain_terms[3], gain_terms[4]), 'shard')  175 us
    unnamed x1, blocking collectives  141 us
  transfers between devices with their start and end apart: 3, of which 0 were waited for; matrix products, arithmetic and copies ran while one was open for 1% of the time, Pallas kernels for 0%

profile of v1, /device:TPU:2, one launch (start us, length us, event | category | flops | bytes accessed | tf_op | source)
XLA Modules:
  0.0 1063.1 jit_solution(15554286908684314314)
XLA Ops:
  7.2 1.1 multiply_reduce_fusion.1
  8.3 1.0 multiply_reduce_fusion.5
  9.3 1.5 multiply_reduce_fusion.2
  10.8 696.8 %all-reduce.1 = (f32[1,2]{1,0:T(1,128)S(1)}, f32[1,2]{1,0:T(1,128)S(1)}, f32[1,2]{1,0:T(1,128)S(1)}, f32[1,2]{1,0:T(1,128)S(1)}, f32[1]{0:T(128)}, /*index=5*/f32[1]{0:T(128)}) all-reduce(f32[1,2]{1,0:T(1,128)S(1)} %bitcast.26, f32[1,2]{1,0:T(1,128)S(1)} %bitcast.25, ...), channel_id=1, replica_groups=mesh['shard'=64,'tensor'=4,'section'=2] {'shard','tensor'}, use_global_device_ids=true, to_apply=%region_3.0 | all-reduce | flops 10 | bytes 80 | tf_op jit(solution)/shard_map/psum | solution.py:60
  707.5 1.5 convert_bitcast_fusion
  709.1 1.6 stack.2
  710.7 0.0 copy-start.11
  710.7 16.2 %all-to-all-start = ((bf16[64,1,2,16,512]{4,3,2,1,0:T(8,128)(2,1)}), bf16[64,1,2,16,512]{4,3,2,1,0:T(8,128)(2,1)S(1)}, u32[]{:S(2)}, u32[]{:S(2)}) async-start(bf16[64,1,2,16,512]{4,3,2,1,0:T(8,128)(2,1)} %stack.2), calls=%async_computation | async-start | bytes 4194304 | tf_op jit(solution)/shard_map/all_to_all | solution.py:74
  726.9 0.0 all-gather.3.cloned.1.call-start
  727.0 0.7 fusion.5
  727.7 0.0 all-gather.3.cloned.1.call-update
  727.7 0.0 all-gather.5.cloned.1.call-start
  729.2 0.6 fusion.4
  729.9 0.0 all-gather.5.cloned.1.call-update
  729.9 1.1 multiply_reduce_fusion.6
  731.1 174.5 %all-reduce.2 = (f32[1]{0:T(128)}, f32[1]{0:T(128)}) all-reduce(f32[1]{0:T(128)} %bitcast.9, f32[1]{0:T(128)} %bitcast.10), channel_id=1, replica_groups=mesh['shard'=64,'tensor'=4,'section'=2] {'shard'}, use_global_device_ids=true, to_apply=%region_13.0 | all-reduce | flops 2 | bytes 16 | tf_op jit(solution)/shard_map/psum | solution.py:63
  907.0 1.3 dynamic-slice
  908.9 0.5 convert_bitcast_fusion.1
  909.5 0.2 dynamic-update-slice
  909.6 141.2 %all-reduce = bf16[1024]{0:T(1024)(128)(2,1)S(1)} all-reduce(bf16[1024]{0:T(1024)(128)(2,1)S(1)} %dynamic-update-slice), channel_id=1, replica_groups=mesh['shard'=64,'tensor'=4,'section'=2] {'shard'}, use_global_device_ids=true, to_apply=%add | all-reduce | flops 1024 | bytes 4096
  1050.8 0.6 reshape.89
  1051.4 2.3 copy.35
  1053.7 1.5 copy.34
  1055.2 1.0 copy.38
  (30 shorter events, 0.1 us)
Async XLA Ops:
  8.3 702.4 %copy-start.1 = (f32[1,2,16,512]{3,2,1,0:T(8,128)}, f32[1,2,16,512]{3,2,1,0:T(8,128)S(1)}, u32[]{:S(2)}) copy-start(f32[1,2,16,512]{3,2,1,0:T(8,128)S(1)} %get-tuple-element.103) | copy-start | bytes 196612
  8.3 702.4 %copy-start.2 = (f32[1,2,16,512]{3,2,1,0:T(8,128)}, f32[1,2,16,512]{3,2,1,0:T(8,128)S(1)}, u32[]{:S(2)}) copy-start(f32[1,2,16,512]{3,2,1,0:T(8,128)S(1)} %get-tuple-element.104) | copy-start | bytes 196612
  9.3 717.7 %copy-start.5 = (f32[1,2,16,256]{3,2,1,0:T(8,128)}, f32[1,2,16,256]{3,2,1,0:T(8,128)S(1)}, u32[]{:S(2)}) copy-start(f32[1,2,16,256]{3,2,1,0:T(8,128)S(1)} %get-tuple-element.100) | copy-start | bytes 98308
  9.3 717.7 %copy-start.6 = (f32[1,2,16,256]{3,2,1,0:T(8,128)}, f32[1,2,16,256]{3,2,1,0:T(8,128)S(1)}, u32[]{:S(2)}) copy-start(f32[1,2,16,256]{3,2,1,0:T(8,128)S(1)} %get-tuple-element.101) | copy-start | bytes 98308
  10.7 718.5 %copy-start.7 = (f32[1,512,16]{1,2,0:T(8,128)}, f32[1,512,16]{1,2,0:T(8,128)S(1)}, u32[]{:S(2)}) copy-start(f32[1,512,16]{1,2,0:T(8,128)S(1)} %get-tuple-element.106) | copy-start | bytes 98308
  10.7 718.5 %copy-start.8 = (f32[1,512,16]{1,2,0:T(8,128)}, f32[1,512,16]{1,2,0:T(8,128)S(1)}, u32[]{:S(2)}) copy-start(f32[1,512,16]{1,2,0:T(8,128)S(1)} %get-tuple-element.107) | copy-start | bytes 98308
  710.7 16.4 %copy-start.3 = (f32[1,2,16,256]{3,2,1,0:T(8,128)S(1)}, f32[1,2,16,256]{3,2,1,0:T(8,128)}, u32[]{:S(2)}) copy-start(f32[1,2,16,256]{3,2,1,0:T(8,128)} %param.16) | copy-start | bytes 98308
  710.7 18.6 %copy-start.4 = (f32[1,512,16]{1,2,0:T(8,128)S(1)}, f32[1,512,16]{1,2,0:T(8,128)}, u32[]{:S(2)}) copy-start(f32[1,512,16]{1,2,0:T(8,128)} %param.24) | copy-start | bytes 98308
  710.7 19.2 %copy-start.9 = (f32[1,16]{1,0:T(1,128)S(1)}, f32[1,16]{1,0:T(1,128)}, u32[]{:S(2)}) copy-start(f32[1,16]{1,0:T(1,128)} %param.28) | copy-start | bytes 196
  710.7 19.3 %copy-start.10 = (f32[1,16]{1,0:T(1,128)S(1)}, f32[1,16]{1,0:T(1,128)}, u32[]{:S(2)}) copy-start(f32[1,16]{1,0:T(1,128)} %param.29) | copy-start | bytes 196
  710.7 19.3 %copy-start.11 = (f32[1,16]{1,0:T(1,128)S(1)}, f32[1,16]{1,0:T(1,128)}, u32[]{:S(2)}) copy-start(f32[1,16]{1,0:T(1,128)} %param.30) | copy-start | bytes 196
  710.7 19.3 %copy-start.12 = (f32[1,16]{1,0:T(1,128)S(1)}, f32[1,16]{1,0:T(1,128)}, u32[]{:S(2)}) copy-start(f32[1,16]{1,0:T(1,128)} %param.31) | copy-start | bytes 196
  710.7 343.0 %all-to-all-start = ((bf16[64,1,2,16,512]{4,3,2,1,0:T(8,128)(2,1)}), bf16[64,1,2,16,512]{4,3,2,1,0:T(8,128)(2,1)S(1)}, u32[]{:S(2)}, u32[]{:S(2)}) async-start(bf16[64,1,2,16,512]{4,3,2,1,0:T(8,128)(2,1)} %stack.2), calls=%async_computation | async-start | bytes 4194304 | tf_op jit(solution)/shard_map/all_to_all | solution.py:74
  726.9 324.5 %all-gather.3.cloned.1.call-start = ((), (), s32[]{:S(2)}) async-start(), calls=%async_computation.1 | async-start | bytes 1064960 | tf_op jit(solution)/shard_map/all_gather | solution.py:72
  727.7 323.7 %all-gather.5.cloned.1.call-start = ((), (), s32[]{:S(2)}) async-start(), calls=%async_computation.2 | async-start | bytes 1064960 | tf_op jit(solution)/shard_map/all_gather | solution.py:76
  1053.7 1.5 copy-start
Sparse Core Ops, SparseCore 0:
  731.3 136.6 all-gather.2
  871.5 133.7 all-gather.4
